TPU v7x, 32 devices: a whole 2x2x4 slice. The times are simulated.
32 devices in a mesh: node: 16 (over z, y, core), chip: 2 (over x).
Axes of the slice: x: 2, y: 2, z: 4, core: 2. Of those that a mesh axis runs over, the one named last changes fastest.
Arguments:
- tokens: bfloat16 [256, 3584], P(('node', 'chip')), may hold values from -6 to 6
- expert_ids: int32 [256, 8], P(('node', 'chip')), may hold values from 0 to 31, as said below
- gate_values: bfloat16 [256, 8], P(('node', 'chip')), may hold values from 0.099609375 to 1
- slot_ids: int32 [256, 8], P(('node', 'chip')), may hold values from 0 to 7, as said below
- up_weight: bfloat16 [32, 3584, 1024], P('node', None, 'chip'), may hold values from -0.09375 to 0.09375
- down_weight: bfloat16 [32, 1024, 3584], P('node', 'chip'), may hold values from -0.1875 to 0.1875
Outputs:
- mixed: bfloat16 [256, 3584], P(('node', 'chip'))
Inputs may be any that keep to these rules, and one draw needn't show every extreme that they name: `expert_ids`: each token's 8 entries name, in some order, all 2 experts of each of 4 distinct nodes. `slot_ids`: entries of one token that name experts of the same node hold the same slot; among the 16 tokens of one node (aligned blocks of the token dimension), the slots to one destination node are distinct, and some destination node receives all 8 slots from each source node.
All inputs are finite; a program needn't handle non-finite values.
Results may differ from a plain program's by a relative error of at most 0.0058.
Values may be sent and summed in bfloat16 or wider, within the bound.
A program may use at most 64 MiB of HBM per device.

v0:
```python
import jax
import jax.numpy as jnp
from jax import lax
from jax.sharding import PartitionSpec as P


def pack_rows(targets, experts, node_tokens, node_gates, row_count, per_node):
    row_ids = jnp.arange(row_count, dtype=jnp.int32)
    matches = (targets[None, :, :] == row_ids[:, None, None]).astype(jnp.bfloat16)
    picked = jnp.minimum(jnp.sum(matches.astype(jnp.float32), axis=2), 1.0).astype(jnp.bfloat16)
    packed = jnp.dot(picked, node_tokens, preferred_element_type=jnp.float32).astype(jnp.bfloat16)
    choose = (experts[:, :, None] == jnp.arange(per_node, dtype=jnp.int32)[None, None, :]).astype(
        jnp.bfloat16
    )
    weighted = choose * node_gates[:, :, None]
    gate_rows = jnp.einsum(
        "rtk,tke->re", matches, weighted, preferred_element_type=jnp.float32
    ).astype(jnp.bfloat16)
    return (packed, gate_rows)


def expert_rows(row_block, gate_block, up_local, down_local):
    result = jnp.zeros((row_block.shape[0], down_local.shape[2]), jnp.float32)
    for expert in range(up_local.shape[0]):
        hidden = jax.nn.silu(
            jnp.dot(row_block, up_local[expert], preferred_element_type=jnp.float32)
        ).astype(jnp.bfloat16)
        product = jnp.dot(hidden, down_local[expert], preferred_element_type=jnp.float32)
        result = result + gate_block[:, expert : expert + 1].astype(jnp.float32) * product
    return result.astype(jnp.bfloat16)


def gather_sum(indices, table):
    valid = indices >= 0
    safe = jnp.where(valid, indices, 0).reshape(-1)
    picked = jnp.take(table, safe, axis=0).reshape(
        indices.shape[0], indices.shape[1], table.shape[1]
    )
    return jnp.sum(jnp.where(valid[:, :, None], picked, 0.0), axis=1)


def shards(tokens, expert_ids, gate_values, slot_ids, up_weight, down_weight):
    node_count = lax.axis_size("node")
    chip_count = lax.axis_size("chip")
    my_chip = lax.axis_index("chip")
    tok_dev = tokens.shape[0]
    model_dim = tokens.shape[1]
    per_node = up_weight.shape[0]
    capacity = 8 * chip_count * tok_dev // node_count
    block_cap = capacity // chip_count
    route_code = (expert_ids // per_node * capacity + slot_ids) * per_node + expert_ids % per_node
    node_tokens, node_gates = (
        lax.all_gather(tokens, "chip", axis=0, tiled=True),
        lax.all_gather(gate_values, "chip", axis=0, tiled=True),
    )
    node_codes = lax.all_gather(route_code, "chip", axis=0, tiled=True)
    node_expert = node_codes % per_node
    node_slot = node_codes // per_node % capacity
    node_dest = node_codes // per_node // capacity
    targets = node_dest * capacity + node_slot
    packed, gate_rows = pack_rows(
        targets, node_expert, node_tokens, node_gates, node_count * capacity, per_node
    )
    shaped = packed.reshape(node_count, chip_count, 1, block_cap, model_dim)
    gate_shaped = gate_rows.reshape(node_count, chip_count, 1, block_cap, per_node)
    arrived, arrived_gates = (
        lax.all_to_all(shaped, "node", split_axis=0, concat_axis=2, tiled=True),
        lax.all_to_all(gate_shaped, "node", split_axis=0, concat_axis=2, tiled=True),
    )
    row_block = arrived.reshape(-1, model_dim)
    gate_block = arrived_gates.reshape(-1, per_node)
    partial_value = expert_rows(row_block, gate_block, up_weight, down_weight)
    pieces = lax.all_to_all(
        partial_value.reshape(chip_count, node_count * block_cap, model_dim),
        "chip",
        split_axis=0,
        concat_axis=0,
        tiled=True,
    )
    slot_sums = jnp.sum(pieces.astype(jnp.float32), axis=0).reshape(
        node_count, block_cap, model_dim
    )
    held = lax.all_to_all(slot_sums, "node", split_axis=0, concat_axis=0, tiled=True).reshape(
        node_count * block_cap, model_dim
    )
    wanted = (node_slot // block_cap == my_chip) & (node_expert == 0)
    indices = jnp.where(wanted, node_dest * block_cap + node_slot % block_cap, -1)
    term = gather_sum(indices, held)
    summed = lax.psum_scatter(term, "chip", scatter_dimension=0, tiled=True)
    return summed.astype(jnp.bfloat16)


def solution(mesh):
    return jax.shard_map(
        shards,
        mesh=mesh,
        in_specs=(
            P(("node", "chip"), None),
            P(("node", "chip"), None),
            P(("node", "chip"), None),
            P(("node", "chip"), None),
            P("node", None, "chip"),
            P("node", "chip", None),
        ),
        out_specs=P(("node", "chip"), None),
        check_vma=False,
    )
```

profile of v0, /device:TPU:0, one launch (start us, length us, event | category | flops | bytes accessed | tf_op | source)
XLA Modules:
  0.0 136.6 jit_solution(9596992641009980675)
XLA Ops:
  6.5 0.7 fusion.38
  7.3 5.3 %all_gather.9 = s32[16,8]{1,0:T(8,128)S(1)} all-gather(s32[8,8]{1,0:T(8,128)S(1)} %fusion.38), channel_id=1, replica_groups=mesh['node'=16,'chip'=2] {'chip'}, dimensions={0}, use_global_device_ids=true | all-gather | bytes 768 | tf_op jit(solution)/shard_map/all_gather | solution.py:56
  12.5 4.6 %all_gather.10 = bf16[16,8]{1,0:T(8,128)(2,1)S(1)} all-gather(bf16[8,8]{1,0:T(8,128)(2,1)} %param.8), channel_id=1, replica_groups=mesh['node'=16,'chip'=2] {'chip'}, dimensions={0}, use_global_device_ids=true | all-gather | bytes 384 | tf_op jit(solution)/shard_map/all_gather | solution.py:54
  17.4 0.2 fusion.14
  17.7 0.6 copy.19
  18.3 6.4 %all-to-all-start = ((bf16[16,2,1,4,2]{3,1,4,2,0:T(2,128)(2,1)}), bf16[16,2,1,4,2]{3,1,4,2,0:T(2,128)(2,1)S(1)}, u32[]{:S(2)}, u32[]{:S(2)}) async-start(bf16[16,2,1,4,2]{3,1,4,2,0:T(2,128)(2,1)} %copy.19), calls=%async_computation | async-start | bytes 32768 | tf_op jit(solution)/shard_map/all_to_all | solution.py:68
  24.8 5.1 %all_gather.11 = bf16[16,3584]{1,0:T(8,128)(2,1)S(1)} all-gather(bf16[8,3584]{1,0:T(8,128)(2,1)} %param.6), channel_id=1, replica_groups=mesh['node'=16,'chip'=2] {'chip'}, dimensions={0}, use_global_device_ids=true | all-gather | bytes 172032 | tf_op jit(solution)/shard_map/all_gather | solution.py:53
  29.9 0.4 convolution_convert_fusion
  30.4 1.1 reshape.72
  31.5 6.0 %all-to-all-start.1 = ((bf16[16,2,1,4,3584]{4,3,1,2,0:T(4,128)(2,1)}), bf16[16,2,1,4,3584]{4,3,1,2,0:T(4,128)(2,1)S(1)}, u32[]{:S(2)}, u32[]{:S(2)}) async-start(bf16[16,2,1,4,3584]{4,3,1,2,0:T(4,128)(2,1)} %bitcast.4), calls=%async_computation.1 | async-start | bytes 1835008 | tf_op jit(solution)/shard_map/all_to_all | solution.py:67
  37.6 20.6 %all-to-all-done.1 = bf16[16,2,1,4,3584]{4,3,1,2,0:T(4,128)(2,1)S(1)} async-done(((bf16[16,2,1,4,3584]{4,3,1,2,0:T(4,128)(2,1)}), bf16[16,2,1,4,3584]{4,3,1,2,0:T(4,128)(2,1)S(1)}, u32[]{:S(2)}, u32[]{:S(2)}) %all-to-all-start.1) | async-done | bytes 917536 | tf_op jit(solution)/shard_map/all_to_all | solution.py:67
  58.3 0.3 copy.22
  58.6 0.2 reshape.73
  58.8 5.7 %convolution_multiply_fusion.1 = f32[128,3584]{1,0:T(8,128)} fusion(bf16[2,512,3584]{2,1,0:T(8,128)(2,1)} %param.11, f32[128]{0:T(128)S(1)} %get-tuple-element.10, bf16[128,3584]{1,0:T(8,128)(2,1)S(1)} %reshape.73, bf16[2,3584,512]{2,1,0:T(8,128)(2,1)} %param.10), kind=kOutput, calls=%fused_computation.3 | convolution fusion | flops 940310528 | bytes 10093056 | tf_op jit(solution)/shard_map/dot_general | solution.py:28
  64.5 4.9 %fusion.1 = bf16[128,3584]{1,0:T(8,128)(2,1)S(1)} fusion(f32[128,3584]{1,0:T(8,128)} %convolution_multiply_fusion.1, bf16[2,512,3584]{2,1,0:T(8,128)(2,1)} %param.11, f32[128]{0:T(128)S(1)} %get-tuple-element.9, bf16[128,3584]{1,0:T(8,128)(2,1)S(1)} %reshape.73, bf16[2,3584,512]{2,1,0:T(8,128)(2,1)} %param.10), kind=kOutput, calls=%fused_computation.4 | convolution fusion | flops 941228032 | bytes 11010560 | tf_op jit(solution)/shard_map/dot_general | solution.py:28
  69.5 15.6 %all_to_all.40 = bf16[2,64,3584]{2,1,0:T(8,128)(2,1)S(1)} all-to-all(bf16[2,64,3584]{2,1,0:T(8,128)(2,1)S(1)} %bitcast.58), channel_id=1, replica_groups=mesh['node'=16,'chip'=2] {'chip'}, dimensions={0} | all-to-all | bytes 1835008 | tf_op jit(solution)/shard_map/all_to_all | solution.py:73
  85.2 1.2 reshape.75
  86.4 5.9 %all-to-all-start.3 = ((f32[16,4,3584]{2,1,0:T(4,128)}), f32[16,4,3584]{2,1,0:T(4,128)S(1)}, u32[]{:S(2)}, u32[]{:S(2)}) async-start(f32[16,4,3584]{2,1,0:T(4,128)} %reshape.75), calls=%async_computation.3 | async-start | bytes 1835008 | tf_op jit(solution)/shard_map/all_to_all | solution.py:83
  92.6 20.5 %all-to-all-done.3 = f32[16,4,3584]{2,1,0:T(4,128)S(1)} async-done(((f32[16,4,3584]{2,1,0:T(4,128)}), f32[16,4,3584]{2,1,0:T(4,128)S(1)}, u32[]{:S(2)}, u32[]{:S(2)}) %all-to-all-start.3) | async-done | bytes 917536 | tf_op jit(solution)/shard_map/all_to_all | solution.py:83
  113.1 0.3 reshape.76
  113.5 1.3 gather_fusion
  114.7 1.4 %fusion.13 = f32[16,3584]{1,0:T(8,128)} fusion(f32[128,3584]{1,0:T(8,128)S(1)} %gather_fusion, pred[16,8]{1,0:T(8,128)(4,1)S(1)} %compare_and_fusion, pred[16,8]{1,0:T(8,128)(4,1)S(1)} %get-tuple-element.5), kind=kLoop, calls=%fused_computation.18 | loop fusion | flops 1318912 | bytes 2064640 | tf_op jit(solution)/shard_map/reduce_sum | solution.py:39
  116.2 12.0 %reduce-scatter.2.cloned.1.call-done = f32[8,3584]{1,0:T(8,128)} async-done(((f32[16,3584]{1,0:T(8,128)}), f32[8,3584]{1,0:T(8,128)}) %reduce-scatter.2.cloned.1.call-update) | async-done | bytes 114704 | tf_op jit(solution)/shard_map/reduce_scatter | solution.py:89
  128.2 1.5 %convert_element_type.42 = bf16[8,3584]{1,0:T(8,128)(2,1)} convert(f32[8,3584]{1,0:T(8,128)} %reduce-scatter.2.cloned.1.call-done) | non-fusion elementwise | flops 28672 | bytes 172032 | tf_op jit(solution)/shard_map/convert_element_type | solution.py:90
  (19 shorter events, 0.9 us)
Async XLA Ops:
  18.3 13.2 %all-to-all-start = ((bf16[16,2,1,4,2]{3,1,4,2,0:T(2,128)(2,1)}), bf16[16,2,1,4,2]{3,1,4,2,0:T(2,128)(2,1)S(1)}, u32[]{:S(2)}, u32[]{:S(2)}) async-start(bf16[16,2,1,4,2]{3,1,4,2,0:T(2,128)(2,1)} %copy.19), calls=%async_computation | async-start | bytes 32768 | tf_op jit(solution)/shard_map/all_to_all | solution.py:68
  31.5 26.8 %all-to-all-start.1 = ((bf16[16,2,1,4,3584]{4,3,1,2,0:T(4,128)(2,1)}), bf16[16,2,1,4,3584]{4,3,1,2,0:T(4,128)(2,1)S(1)}, u32[]{:S(2)}, u32[]{:S(2)}) async-start(bf16[16,2,1,4,3584]{4,3,1,2,0:T(4,128)(2,1)} %bitcast.4), calls=%async_computation.1 | async-start | bytes 1835008 | tf_op jit(solution)/shard_map/all_to_all | solution.py:67
  86.4 26.7 %all-to-all-start.3 = ((f32[16,4,3584]{2,1,0:T(4,128)}), f32[16,4,3584]{2,1,0:T(4,128)S(1)}, u32[]{:S(2)}, u32[]{:S(2)}) async-start(f32[16,4,3584]{2,1,0:T(4,128)} %reshape.75), calls=%async_computation.3 | async-start | bytes 1835008 | tf_op jit(solution)/shard_map/all_to_all | solution.py:83
  92.4 35.9 %reduce-scatter.2.cloned.1.call-start = ((), (), s32[]{:S(2)}) async-start(), calls=%async_computation.5 | async-start | bytes 344064 | tf_op jit(solution)/shard_map/reduce_scatter | solution.py:89
Sparse Core Ops, SparseCore 0:
  116.3 11.8 reduce-scatter.1
where the time goes:
time: 137 us
  waiting for transfers between devices  53.3 us (39%)
  blocking collectives  30.6 us (22%)
  starting transfers between devices  18.4 us (13%)
  between operations  13.5 us (10%)
  matrix products  11.3 us (8%)
  local copies, waits for them, and re-layouts  5.6 us (4%)
  other arithmetic  3.99 us (3%)
    all_to_all x1, waiting for transfers between devices, shards(): lax.all_to_all(shaped, 'node', split_axis=0, concat_axis=2, tiled=True)  20.6 us
    all_to_all x1, waiting for transfers between devices, shards(): lax.all_to_all(slot_sums, 'node', split_axis=0, concat_axis=0, tiled=True)  20.5 us
    all_to_all x1, blocking collectives, shards(): lax.all_to_all(partial_value.reshape(chip_count, node_count * block_cap,...  15.6 us
    reduce_scatter x1, waiting for transfers between devices, shards(): summed = lax.psum_scatter(term, 'chip', scatter_dimension=0, tiled=True)  12 us
    dot_general x2, matrix products, expert_rows(): jnp.dot(hidden, down_local[expert], preferred_element_type=jnp.float32)  10.7 us
    all_to_all x1, starting transfers between devices, shards(): lax.all_to_all(gate_shaped, 'node', split_axis=0, concat_axis=2, tiled=True)  6.42 us
    all_to_all x1, starting transfers between devices, shards(): lax.all_to_all(shaped, 'node', split_axis=0, concat_axis=2, tiled=True)  5.97 us
    all_to_all x1, starting transfers between devices, shards(): lax.all_to_all(slot_sums, 'node', split_axis=0, concat_axis=0, tiled=True)  5.95 us
  transfers between devices with their start and end apart: 4, of which 3 were waited for; matrix products, arithmetic and copies ran while one was open for 1% of the time, Pallas kernels for 0%

commit v1 on v0

--- a/solution.py
+++ b/solution.py
@@ -64,7 +64,12 @@
     shaped = packed.reshape(node_count, chip_count, 1, block_cap, model_dim)
     gate_shaped = gate_rows.reshape(node_count, chip_count, 1, block_cap, per_node)
     arrived, arrived_gates = (
-        lax.all_to_all(shaped, "node", split_axis=0, concat_axis=2, tiled=True),
+        jnp.concatenate(
+            lax.all_to_all(
+                jnp.stack(jnp.split(shaped, lax.axis_size("node"), axis=0)), "node", 0, 0
+            ),
+            axis=2,
+        ),
         lax.all_to_all(gate_shaped, "node", split_axis=0, concat_axis=2, tiled=True),
     )
     row_block = arrived.reshape(-1, model_dim)

time: 137 us -> 147 us (1.073)
  local copies, waits for them, and re-layouts: 5.6 us -> 15.1 us
    unnamed x0 -> x15, local copies, waits for them, and re-layouts: none -> 9.59 us
  transfers between devices with their start and end apart: 4 -> 4, of which waited for: 3 -> 3; matrix products, arithmetic and copies ran while one was open for 1% -> 8% of each run, Pallas kernels for 0% -> 0%
where the time goes in v1:
time: 147 us; the launch traced here: 146 us
  waiting for transfers between devices  53.3 us (36%)
  blocking collectives  30.6 us (21%)
  starting transfers between devices  18.4 us (13%)
  local copies, waits for them, and re-layouts  15.1 us (10%)
  between operations  13.6 us (9%)
  matrix products  11.3 us (8%)
  other arithmetic  4 us (3%)
    all_to_all x1, waiting for transfers between devices, shards(): lax.all_to_all(jnp.stack(jnp.split(shaped, lax.axis_size('node'), axis=0)...  20.6 us
    all_to_all x1, waiting for transfers between devices, shards(): lax.all_to_all(slot_sums, 'node', split_axis=0, concat_axis=0, tiled=True)  20.5 us
    all_to_all x1, blocking collectives, shards(): lax.all_to_all(partial_value.reshape(chip_count, node_count * block_cap,...  15.6 us
    reduce_scatter x1, waiting for transfers between devices, shards(): summed = lax.psum_scatter(term, 'chip', scatter_dimension=0, tiled=True)  12 us
    dot_general x2, matrix products, expert_rows(): jnp.dot(hidden, down_local[expert], preferred_element_type=jnp.float32)  10.7 us
    unnamed x15, local copies, waits for them, and re-layouts  9.59 us
    all_to_all x1, starting transfers between devices, shards(): lax.all_to_all(gate_shaped, 'node', split_axis=0, concat_axis=2, tiled=True)  6.42 us
    all_to_all x1, starting transfers between devices, shards(): lax.all_to_all(jnp.stack(jnp.split(shaped, lax.axis_size('node'), axis=0)...  5.97 us
  transfers between devices with their start and end apart: 4, of which 3 were waited for; matrix products, arithmetic and copies ran while one was open for 8% of the time, Pallas kernels for 0%

profile of v1, /device:TPU:0, one launch (start us, length us, event | category | flops | bytes accessed | tf_op | source)
XLA Modules:
  0.0 146.2 jit_solution(2274132439537289467)
XLA Ops:
  6.5 0.7 fusion.38
  7.3 5.3 %all_gather.9 = s32[16,8]{1,0:T(8,128)S(1)} all-gather(s32[8,8]{1,0:T(8,128)S(1)} %fusion.38), channel_id=1, replica_groups=mesh['node'=16,'chip'=2] {'chip'}, dimensions={0}, use_global_device_ids=true | all-gather | bytes 768 | tf_op jit(solution)/shard_map/all_gather | solution.py:56
  12.5 4.6 %all_gather.10 = bf16[16,8]{1,0:T(8,128)(2,1)S(1)} all-gather(bf16[8,8]{1,0:T(8,128)(2,1)} %param.8), channel_id=1, replica_groups=mesh['node'=16,'chip'=2] {'chip'}, dimensions={0}, use_global_device_ids=true | all-gather | bytes 384 | tf_op jit(solution)/shard_map/all_gather | solution.py:54
  18.3 6.4 %all-to-all-start = ((bf16[16,2,1,4,2]{3,1,4,2,0:T(2,128)(2,1)}), bf16[16,2,1,4,2]{3,1,4,2,0:T(2,128)(2,1)S(1)}, u32[]{:S(2)}, u32[]{:S(2)}) async-start(bf16[16,2,1,4,2]{3,1,4,2,0:T(2,128)(2,1)} %copy.34), calls=%async_computation | async-start | bytes 32768 | tf_op jit(solution)/shard_map/all_to_all | solution.py:73
  24.8 5.1 %all_gather.11 = bf16[16,3584]{1,0:T(8,128)(2,1)S(1)} all-gather(bf16[8,3584]{1,0:T(8,128)(2,1)} %param.6), channel_id=1, replica_groups=mesh['node'=16,'chip'=2] {'chip'}, dimensions={0}, use_global_device_ids=true | all-gather | bytes 172032 | tf_op jit(solution)/shard_map/all_gather | solution.py:53
  32.7 0.6 constant_dynamic-update-slice_fusion.12
  34.0 0.7 constant_dynamic-update-slice_fusion.10
  34.6 0.6 constant_dynamic-update-slice_fusion.9
  36.6 0.7 constant_dynamic-update-slice_fusion.6
  37.2 0.6 constant_dynamic-update-slice_fusion.5
  39.8 0.7 constant_dynamic-update-slice_fusion.1
  40.4 0.6 constant_dynamic-update-slice_fusion
  41.1 6.0 %all-to-all-start.1 = ((bf16[16,1,2,1,4,3584]{5,4,2,3,1,0:T(4,128)(2,1)}), bf16[16,1,2,1,4,3584]{5,4,2,3,1,0:T(4,128)(2,1)S(1)}, u32[]{:S(2)}, u32[]{:S(2)}) async-start(bf16[16,1,2,1,4,3584]{5,4,2,3,1,0:T(4,128)(2,1)} %constant_dynamic-update-slice_fusion), calls=%async_computation.1 | async-start | bytes 1835008 | tf_op jit(solution)/shard_map/all_to_all | solution.py:68
  47.2 20.6 %all-to-all-done.1 = bf16[16,1,2,1,4,3584]{5,4,2,3,1,0:T(4,128)(2,1)S(1)} async-done(((bf16[16,1,2,1,4,3584]{5,4,2,3,1,0:T(4,128)(2,1)}), bf16[16,1,2,1,4,3584]{5,4,2,3,1,0:T(4,128)(2,1)S(1)}, u32[]{:S(2)}, u32[]{:S(2)}) %all-to-all-start.1) | async-done | bytes 917536 | tf_op jit(solution)/shard_map/all_to_all | solution.py:68
  68.3 5.7 %convolution_multiply_fusion.1 = f32[128,3584]{1,0:T(8,128)} fusion(bf16[2,512,3584]{2,1,0:T(8,128)(2,1)} %param.11, f32[128]{0:T(128)S(1)} %get-tuple-element.26, bf16[128,3584]{1,0:T(8,128)(2,1)S(1)} %reshape_reshape.3, bf16[2,3584,512]{2,1,0:T(8,128)(2,1)} %param.10), kind=kOutput, calls=%fused_computation.3 | convolution fusion | flops 940310528 | bytes 10093056 | tf_op jit(solution)/shard_map/dot_general | solution.py:28
  74.1 5.0 %fusion.1 = bf16[128,3584]{1,0:T(8,128)(2,1)S(1)} fusion(f32[128,3584]{1,0:T(8,128)} %convolution_multiply_fusion.1, bf16[2,512,3584]{2,1,0:T(8,128)(2,1)} %param.11, f32[128]{0:T(128)S(1)} %get-tuple-element.25, bf16[128,3584]{1,0:T(8,128)(2,1)S(1)} %reshape_reshape.3, bf16[2,3584,512]{2,1,0:T(8,128)(2,1)} %param.10), kind=kOutput, calls=%fused_computation.4 | convolution fusion | flops 941228032 | bytes 11010560 | tf_op jit(solution)/shard_map/dot_general | solution.py:28
  79.0 15.6 %all_to_all.30 = bf16[2,64,3584]{2,1,0:T(8,128)(2,1)S(1)} all-to-all(bf16[2,64,3584]{2,1,0:T(8,128)(2,1)S(1)} %bitcast.55), channel_id=1, replica_groups=mesh['node'=16,'chip'=2] {'chip'}, dimensions={0} | all-to-all | bytes 1835008 | tf_op jit(solution)/shard_map/all_to_all | solution.py:78
  94.8 1.2 reshape.103
  96.0 5.9 %all-to-all-start.3 = ((f32[16,4,3584]{2,1,0:T(4,128)}), f32[16,4,3584]{2,1,0:T(4,128)S(1)}, u32[]{:S(2)}, u32[]{:S(2)}) async-start(f32[16,4,3584]{2,1,0:T(4,128)} %reshape.103), calls=%async_computation.3 | async-start | bytes 1835008 | tf_op jit(solution)/shard_map/all_to_all | solution.py:88
  102.1 20.5 %all-to-all-done.3 = f32[16,4,3584]{2,1,0:T(4,128)S(1)} async-done(((f32[16,4,3584]{2,1,0:T(4,128)}), f32[16,4,3584]{2,1,0:T(4,128)S(1)}, u32[]{:S(2)}, u32[]{:S(2)}) %all-to-all-start.3) | async-done | bytes 917536 | tf_op jit(solution)/shard_map/all_to_all | solution.py:88
  123.0 1.3 gather_fusion
  124.3 1.4 fusion.13
  125.8 12.0 %reduce-scatter.2.cloned.1.call-done = f32[8,3584]{1,0:T(8,128)} async-done(((f32[16,3584]{1,0:T(8,128)}), f32[8,3584]{1,0:T(8,128)}) %reduce-scatter.2.cloned.1.call-update) | async-done | bytes 114704 | tf_op jit(solution)/shard_map/reduce_scatter | solution.py:94
  137.8 1.5 %convert_element_type.42 = bf16[8,3584]{1,0:T(8,128)(2,1)} convert(f32[8,3584]{1,0:T(8,128)} %reduce-scatter.2.cloned.1.call-done) | non-fusion elementwise | flops 28672 | bytes 172032 | tf_op jit(solution)/shard_map/convert_element_type | solution.py:95
  (51 shorter events, 9.1 us)
Async XLA Ops:
  18.3 22.7 %all-to-all-start = ((bf16[16,2,1,4,2]{3,1,4,2,0:T(2,128)(2,1)}), bf16[16,2,1,4,2]{3,1,4,2,0:T(2,128)(2,1)S(1)}, u32[]{:S(2)}, u32[]{:S(2)}) async-start(bf16[16,2,1,4,2]{3,1,4,2,0:T(2,128)(2,1)} %copy.34), calls=%async_computation | async-start | bytes 32768 | tf_op jit(solution)/shard_map/all_to_all | solution.py:73
  41.1 26.8 %all-to-all-start.1 = ((bf16[16,1,2,1,4,3584]{5,4,2,3,1,0:T(4,128)(2,1)}), bf16[16,1,2,1,4,3584]{5,4,2,3,1,0:T(4,128)(2,1)S(1)}, u32[]{:S(2)}, u32[]{:S(2)}) async-start(bf16[16,1,2,1,4,3584]{5,4,2,3,1,0:T(4,128)(2,1)} %constant_dynamic-update-slice_fusion), calls=%async_computation.1 | async-start | bytes 1835008 | tf_op jit(solution)/shard_map/all_to_all | solution.py:68
  96.0 26.7 %all-to-all-start.3 = ((f32[16,4,3584]{2,1,0:T(4,128)}), f32[16,4,3584]{2,1,0:T(4,128)S(1)}, u32[]{:S(2)}, u32[]{:S(2)}) async-start(f32[16,4,3584]{2,1,0:T(4,128)} %reshape.103), calls=%async_computation.3 | async-start | bytes 1835008 | tf_op jit(solution)/shard_map/all_to_all | solution.py:88
  101.9 35.9 %reduce-scatter.2.cloned.1.call-start = ((), (), s32[]{:S(2)}) async-start(), calls=%async_computation.5 | async-start | bytes 344064 | tf_op jit(solution)/shard_map/reduce_scatter | solution.py:94
Sparse Core Ops, SparseCore 0:
  125.9 11.8 reduce-scatter.1
